TPU v7x, 128 devices: a whole 4x4x4 slice. The times are simulated.
128 devices in a mesh: dp: 4 (over x_lo, core), tensor: 32 (over y, x_hi, z).
Axes of the slice: x: 4 (x_hi: 2, x_lo: 2; x = x_hi * 2 + x_lo), y: 4, z: 4, core: 2. Of those that a mesh axis runs over, the one named last changes fastest.
Arguments:
- qkv_master: float32 [7168, 21504], P(('dp', 'tensor')), may hold values from -0.0625 to 0.0625
- adapter_down: float32 [13, 7168, 128], P(None, ('dp', 'tensor')), may hold values from -0.0625 to 0.0625
- adapter_up: float32 [13, 128, 21504], P(None, None, 'tensor'), may hold values from -0.5 to 0.5
- adapter_pick: int32 [1], replicated, may hold values from 0 to 12
- out_master: float32 [3584, 7168], P(('dp', 'tensor')), may hold values from -0.0625 to 0.0625
- norm_gain: float32 [7168], replicated, may hold values from 0.1 to 1.9
- hidden_in: bfloat16 [2048, 3584], P(('dp', 'tensor')), may hold values from -6 to 6
- embed_in: bfloat16 [2048, 3584], P(('dp', 'tensor')), may hold values from -6 to 6
- prompt_len: int32 [4, 2], P('dp'), may hold values from 1 to 511, as said below
- prefix_len: int32 [4, 2], P('dp'), may hold values from 0 to 512, as said below
- prefix_holder: int32 [4, 2], P('dp'), may hold values from 0 to 3
- prefix_keys: bfloat16 [4, 512, 7168], P('dp', None, 'tensor'), may hold values from -6 to 6
- prefix_values: bfloat16 [4, 512, 7168], P('dp', None, 'tensor'), may hold values from -6 to 6
Outputs:
- server_qkv: bfloat16 [7168, 21504], P(None, 'tensor')
- server_out: bfloat16 [3584, 7168], P(None, 'tensor')
- block_out: bfloat16 [2048, 3584], P(('dp', 'tensor'))
- new_keys: bfloat16 [2048, 7168], P('dp', 'tensor')
- new_values: bfloat16 [2048, 7168], P('dp', 'tensor')
Inputs may be any that keep to these rules, and one draw needn't show every extreme that they name: `prompt_len`: the two prompt lengths of a replica add up to 512. `prefix_len`: exactly half of all requests extend a cached prefix (a positive length); the others have 0.
All inputs are finite; a program needn't handle non-finite values.
Results may differ from a plain program's by a relative error of at most 0.033.
Values may be sent and summed in bfloat16 or wider, within the bound.
A program may use at most 128 MiB of HBM per device.

v0:
```python
import math
import jax
import jax.numpy as jnp
from jax import lax
from jax.sharding import PartitionSpec as P


def partial_attention(queries, key_rows, value_rows, allowed, inv_scale):
    scores = (
        lax.dot_general(
            queries, key_rows, (((1,), (1,)), ((), ())), preferred_element_type=jnp.float32
        )
        * inv_scale
    )
    weights = jnp.where(allowed, jnp.exp(scores), jnp.float32(0.0))
    numerator = jnp.dot(
        weights.astype(jnp.bfloat16), value_rows, preferred_element_type=jnp.float32
    )
    return (numerator, jnp.sum(weights, axis=1))


def regroup_rows(columns, n_tensor, n_replica):
    col_count = columns.shape[1]
    row_count = columns.shape[0] // (n_tensor * n_replica)
    shaped = columns.reshape(n_tensor, n_replica, row_count, col_count)
    return jnp.transpose(shaped, (1, 0, 2, 3)).reshape(n_tensor * n_replica * row_count, col_count)


def body(
    qkv_master,
    adapter_down,
    adapter_up,
    adapter_pick,
    out_master,
    norm_gain,
    hidden_in,
    embed_in,
    prompt_len,
    prefix_len,
    prefix_holder,
    prefix_keys,
    prefix_values,
):
    n_tensor = lax.axis_size("tensor")
    n_replica = lax.axis_size("dp")
    chosen = adapter_pick[0]
    down_pick = lax.dynamic_index_in_dim(adapter_down, chosen, 0, keepdims=False).astype(
        jnp.bfloat16
    )
    up_pick = lax.dynamic_index_in_dim(adapter_up, chosen, 0, keepdims=False).astype(jnp.bfloat16)
    joined = jnp.concatenate([hidden_in, embed_in], axis=1).astype(jnp.float32)
    factor = lax.rsqrt(jnp.mean(joined * joined, axis=1, keepdims=True) + 1e-05)
    normed = (joined * factor * norm_gain).astype(jnp.bfloat16)
    all_rows, up_full = (
        lax.all_gather(normed, "tensor", axis=0, tiled=True),
        lax.all_gather(up_pick, "tensor", axis=1, tiled=True),
    )
    merged_qkv = (
        qkv_master + jnp.dot(down_pick, up_full, preferred_element_type=jnp.float32)
    ).astype(jnp.bfloat16)
    out_low = out_master.astype(jnp.bfloat16)
    rows_qkv, rows_out = (
        lax.all_gather(merged_qkv, "dp", axis=0, tiled=True),
        lax.all_gather(out_low, "dp", axis=0, tiled=True),
    )
    cols_qkv, cols_out = (
        lax.all_to_all(rows_qkv, "tensor", split_axis=1, concat_axis=0, tiled=True),
        lax.all_to_all(rows_out, "tensor", split_axis=1, concat_axis=0, tiled=True),
    )
    server_qkv = regroup_rows(cols_qkv, n_tensor, n_replica)
    server_out = regroup_rows(cols_out, n_tensor, n_replica)
    qkv_rows = jnp.dot(all_rows, server_qkv, preferred_element_type=jnp.float32).astype(
        jnp.bfloat16
    )
    head_size = qkv_rows.shape[1] // 3
    token_count = qkv_rows.shape[0]
    queries = qkv_rows[:, :head_size]
    new_keys = qkv_rows[:, head_size : 2 * head_size]
    new_values = qkv_rows[:, 2 * head_size :]
    inv_scale = 1.0 / math.sqrt(head_size)
    positions = jnp.arange(token_count, dtype=jnp.int32)
    lengths = prompt_len[0]
    request = (positions >= lengths[0]).astype(jnp.int32)
    block_rows = math.gcd(token_count, 512)
    first_row = 0
    last_row = first_row + block_rows
    allowed = (request[first_row:last_row, None] == request[None, :]) & (
        positions[None, :] <= positions[first_row:last_row, None]
    )
    numerator, weight_sum = partial_attention(queries, new_keys, new_values, allowed, inv_scale)
    own_parts = numerator
    own_sums = weight_sum
    cached_len = prefix_len[0]
    holders = prefix_holder[0]
    row_holder = jnp.where(request == 1, holders[1], holders[0])
    row_limit = jnp.where(request == 1, cached_len[1], cached_len[0])
    slot_ids = jnp.arange(prefix_keys.shape[1], dtype=jnp.int32)
    offset = jnp.int32(0)
    numerator = own_parts
    weight_sum = own_sums
    key_piece = lax.all_gather(prefix_keys, "dp", axis=0, tiled=True)
    value_piece = lax.all_gather(prefix_values, "dp", axis=0, tiled=True)
    for member in range(key_piece.shape[0]):
        replica = offset + member
        first_row = 0
        last_row = first_row + block_rows
        usable = (row_holder[first_row:last_row, None] == replica) & (
            slot_ids[None, :] < row_limit[first_row:last_row, None]
        )
        part_num, part_sum = partial_attention(
            queries, key_piece[member], value_piece[member], usable, inv_scale
        )
        numerator = numerator + part_num
        weight_sum = weight_sum + part_sum
    numerator, weight_sum = (numerator, weight_sum)
    attention = (numerator / weight_sum[:, None]).astype(jnp.bfloat16)
    block_out = lax.psum_scatter(
        lax.dot_general(
            attention, server_out, (((1,), (1,)), ((), ())), preferred_element_type=jnp.float32
        ).astype(jnp.bfloat16),
        "tensor",
        scatter_dimension=0,
        tiled=True,
    )
    return (server_qkv, server_out, block_out, new_keys, new_values)


def solution(mesh):
    in_specs = (
        P(("dp", "tensor"), None),
        P(None, ("dp", "tensor"), None),
        P(None, None, "tensor"),
        P(),
        P(("dp", "tensor"), None),
        P(),
        P(("dp", "tensor"), None),
        P(("dp", "tensor"), None),
        P("dp", None),
        P("dp", None),
        P("dp", None),
        P("dp", None, "tensor"),
        P("dp", None, "tensor"),
    )
    out_specs = (
        P(None, "tensor"),
        P(None, "tensor"),
        P(("dp", "tensor"), None),
        P("dp", "tensor"),
        P("dp", "tensor"),
    )
    return jax.shard_map(body, mesh=mesh, in_specs=in_specs, out_specs=out_specs, check_vma=False)
```

profile of v0, /device:TPU:0, one launch (start us, length us, event | category | flops | bytes accessed | tf_op | source)
XLA Modules:
  0.0 744.3 jit_solution(5909597050961547122)
XLA Ops:
  7.9 1.7 dynamic-slice_convert_fusion
  9.7 2.0 convert_bitcast_fusion
  11.8 90.2 %all-gather.11.cloned.1.call-done = bf16[1,128,21504]{1,2,0:T(8,128)(2,1)} async-done(((bf16[1,128,672]{1,2,0:T(8,128)(2,1)}), bf16[1,128,21504]{1,2,0:T(8,128)(2,1)}) %all-gather.11.cloned.1.call-update) | async-done | bytes 5505040 | tf_op jit(solution)/shard_map/all_gather | solution.py:56
  101.9 8.7 %fusion = bf16[56,21504]{1,0:T(8,128)(2,1)} fusion(f32[56,21504]{1,0:T(8,128)} %param.13, bf16[1,128,21504]{1,2,0:T(8,128)(2,1)} %all-gather.11.cloned.1.call-done, f32[13,56,128]{2,1,0:T(8,128)S(1)} %copy-done, s32[]{:T(128)S(6)} %select_n.46), kind=kOutput, calls=%fused_computation.1 | convolution fusion | flops 310689792 | bytes 12744708 | tf_op jit(solution)/shard_map/dot_general | solution.py:59
  111.0 0.8 fusion.28
  111.8 17.1 %all-gather.13.cloned.1.call-done = bf16[4,28,7168]{2,1,0:T(8,128)(2,1)} async-done(((bf16[1,28,7168]{2,1,0:T(8,128)(2,1)}), bf16[4,28,7168]{2,1,0:T(8,128)(2,1)}) %all-gather.13.cloned.1.call-update) | async-done | bytes 1605648 | tf_op jit(solution)/shard_map/all_gather | solution.py:64
  128.9 3.7 all_to_all.27
  132.6 2.3 copy.29
  134.9 9.4 %all-to-all-start.1 = ((bf16[112,32,224]{2,0,1:T(8,128)(2,1)}), bf16[112,32,224]{2,0,1:T(8,128)(2,1)S(1)}, u32[]{:S(2)}, u32[]{:S(2)}) async-start(bf16[112,32,224]{2,0,1:T(8,128)(2,1)} %copy.29), calls=%async_computation.1 | async-start | bytes 3670016 | tf_op jit(solution)/shard_map/all_to_all | solution.py:68
  144.3 97.9 %all-gather.7.cloned.1.call-done = bf16[224,21504]{1,0:T(8,128)(2,1)} async-done(((bf16[56,21504]{1,0:T(8,128)(2,1)}), bf16[224,21504]{1,0:T(8,128)(2,1)}) %all-gather.7.cloned.1.call-update) | async-done | bytes 9633808 | tf_op jit(solution)/shard_map/all_gather | solution.py:63
  242.2 20.8 %all_to_all.24 = bf16[224,32,672]{2,1,0:T(8,128)(2,1)} reshape(bf16[224,21504]{1,0:T(8,128)(2,1)} %all-gather.7.cloned.1.call-done) | data formatting | bytes 19267584 | tf_op jit(solution)/shard_map/all_to_all | solution.py:67
  263.1 11.6 %copy.27 = bf16[224,32,672]{2,0,1:T(8,128)(2,1)} copy(bf16[224,32,672]{2,1,0:T(8,128)(2,1)} %all_to_all.24) | data formatting | bytes 19267584 | tf_op jit(solution)/shard_map/all_to_all | solution.py:67
  274.8 10.4 %all-to-all-start = ((bf16[224,32,672]{2,0,1:T(8,128)(2,1)}), bf16[224,32,672]{2,0,1:T(8,128)(2,1)}, u32[]{:S(2)}, u32[]{:S(2)}) async-start(bf16[224,32,672]{2,0,1:T(8,128)(2,1)} %copy.27), calls=%async_computation | async-start | bytes 22020096 | tf_op jit(solution)/shard_map/all_to_all | solution.py:67
  285.2 0.6 fusion.40
  285.8 1.3 select_compare_fusion
  287.1 1.3 select_compare_fusion.2
  288.5 0.6 fusion.41
  289.1 1.3 broadcast_select_fusion
  290.4 194.6 %all_gather.22 = bf16[4,512,224]{1,2,0:T(8,128)(2,1)} all-gather(bf16[1,512,224]{1,2,0:T(8,128)(2,1)S(1)} %copy-done.7), channel_id=1, replica_groups=mesh['dp'=4,'tensor'=32] {'dp'}, dimensions={0}, use_global_device_ids=true | all-gather | bytes 1146880 | tf_op jit(solution)/shard_map/all_gather | solution.py:101
  485.0 11.8 %all_gather.23 = bf16[4,512,224]{1,2,0:T(8,128)(2,1)S(1)} all-gather(bf16[1,512,224]{1,2,0:T(8,128)(2,1)S(1)} %copy-done.8), channel_id=1, replica_groups=mesh['dp'=4,'tensor'=32] {'dp'}, dimensions={0}, use_global_device_ids=true | all-gather | bytes 1146880 | tf_op jit(solution)/shard_map/all_gather | solution.py:102
  496.8 0.7 copy.30
  497.4 2.4 copy.31
  499.8 2.8 reshape.99
  502.6 9.8 %copy.28 = bf16[4,32,56,672]{3,2,1,0:T(8,128)(2,1)} copy(bf16[4,32,56,672]{3,2,0,1:T(8,128)(2,1)} %bitcast.5) | data formatting | bytes 19267584 | tf_op jit(solution)/shard_map/transpose | solution.py:26
  512.5 13.6 %convolution_convert_fusion.1 = bf16[512,672]{0,1:T(8,128)(2,1)S(1)} fusion(bf16[512,7168]{1,0:T(8,128)(2,1)} %all-gather.9.cloned.1.call-done, bf16[7168,672]{1,0:T(8,128)(2,1)} %bitcast.72), kind=kOutput, calls=%fused_computation.19 | convolution fusion | flops 4932845568 | bytes 17661952 | tf_op jit(solution)/shard_map/dot_general | solution.py:72
  526.1 1.3 fusion.42
  528.5 0.5 fusion.46
  530.4 1.1 convolution_add_fusion.2
  531.5 4.6 convolution_convert_fusion
  536.1 2.5 copy.33
  538.6 13.5 %copy.32 = bf16[7168,672]{0,1:T(8,128)(2,1)} copy(bf16[7168,672]{1,0:T(8,128)(2,1)} %bitcast.73) | data formatting | bytes 19267584
  552.0 185.8 %reduce-scatter.2.cloned.1.call-done = bf16[16,3584]{1,0:T(8,128)(2,1)} async-done(((bf16[512,3584]{1,0:T(8,128)(2,1)}), bf16[16,3584]{1,0:T(8,128)(2,1)}) %reduce-scatter.2.cloned.1.call-update) | async-done | bytes 114704 | tf_op jit(solution)/shard_map/reduce_scatter | solution.py:117
  (50 shorter events, 3.0 us)
Async XLA Ops:
  7.2 94.8 %copy-start = (f32[13,56,128]{2,1,0:T(8,128)S(1)}, f32[13,56,128]{2,1,0:T(8,128)}, u32[]{:S(2)}) copy-start(f32[13,56,128]{2,1,0:T(8,128)} %param.14) | copy-start | bytes 1118212
  7.2 94.7 %all-gather.11.cloned.1.call-start = ((), (), s32[]{:S(2)}) async-start(), calls=%async_computation.6 | async-start | bytes 5677056 | tf_op jit(solution)/shard_map/all_gather | solution.py:56
  9.6 119.3 %all-gather.13.cloned.1.call-start = ((), (), s32[]{:S(2)}) async-start(), calls=%async_computation.7 | async-start | bytes 2293760 | tf_op jit(solution)/shard_map/all_gather | solution.py:64
  11.7 99.1 %copy-start.4 = (bf16[16,3584]{1,0:T(8,128)(2,1)S(1)}, bf16[16,3584]{1,0:T(8,128)(2,1)}, u32[]{:S(2)}) copy-start(bf16[16,3584]{1,0:T(8,128)(2,1)} %param.20) | copy-start | bytes 344068
  11.7 99.1 %copy-start.5 = (bf16[16,3584]{1,0:T(8,128)(2,1)S(1)}, bf16[16,3584]{1,0:T(8,128)(2,1)}, u32[]{:S(2)}) copy-start(bf16[16,3584]{1,0:T(8,128)(2,1)} %param.19) | copy-start | bytes 344068
  11.7 99.2 %copy-start.9 = (f32[7168]{0:T(1024)S(1)}, f32[7168]{0:T(1024)}, u32[]{:S(2)}) copy-start(f32[7168]{0:T(1024)} %param.18) | copy-start | bytes 86020
  11.7 230.5 %all-gather.7.cloned.1.call-start = ((), (), s32[]{:S(2)}) async-start(), calls=%async_computation.3 | async-start | bytes 12042240 | tf_op jit(solution)/shard_map/all_gather | solution.py:63
  110.7 401.8 %all-gather.9.cloned.1.call-start = ((), (), s32[]{:S(2)}) async-start(), calls=%async_computation.4 | async-start | bytes 7569408 | tf_op jit(solution)/shard_map/all_gather | solution.py:55
  134.9 139.8 %all-to-all-start.1 = ((bf16[112,32,224]{2,0,1:T(8,128)(2,1)}), bf16[112,32,224]{2,0,1:T(8,128)(2,1)S(1)}, u32[]{:S(2)}, u32[]{:S(2)}) async-start(bf16[112,32,224]{2,0,1:T(8,128)(2,1)} %copy.29), calls=%async_computation.1 | async-start | bytes 3670016 | tf_op jit(solution)/shard_map/all_to_all | solution.py:68
  274.7 10.5 %copy-start.11 = (s32[1,2]{1,0:T(1,128)S(1)}, s32[1,2]{1,0:T(1,128)}, u32[]{:S(2)}) copy-start(s32[1,2]{1,0:T(1,128)} %param.23) | copy-start | bytes 28
  274.7 11.1 %copy-start.10 = (s32[1,2]{1,0:T(1,128)S(1)}, s32[1,2]{1,0:T(1,128)}, u32[]{:S(2)}) copy-start(s32[1,2]{1,0:T(1,128)} %param.21) | copy-start | bytes 28
  274.7 13.8 %copy-start.12 = (s32[1,2]{1,0:T(1,128)S(1)}, s32[1,2]{1,0:T(1,128)}, u32[]{:S(2)}) copy-start(s32[1,2]{1,0:T(1,128)} %param.22) | copy-start | bytes 28
  274.7 15.7 %copy-start.7 = (bf16[1,512,224]{1,2,0:T(8,128)(2,1)S(1)}, bf16[1,512,224]{1,2,0:T(8,128)(2,1)}, u32[]{:S(2)}) copy-start(bf16[1,512,224]{1,2,0:T(8,128)(2,1)} %param.24) | copy-start | bytes 688132
  274.7 210.2 %copy-start.8 = (bf16[1,512,224]{1,2,0:T(8,128)(2,1)S(1)}, bf16[1,512,224]{1,2,0:T(8,128)(2,1)}, u32[]{:S(2)}) copy-start(bf16[1,512,224]{1,2,0:T(8,128)(2,1)} %param.25) | copy-start | bytes 688132
  274.8 227.9 %all-to-all-start = ((bf16[224,32,672]{2,0,1:T(8,128)(2,1)}), bf16[224,32,672]{2,0,1:T(8,128)(2,1)}, u32[]{:S(2)}, u32[]{:S(2)}) async-start(bf16[224,32,672]{2,0,1:T(8,128)(2,1)} %copy.27), calls=%async_computation | async-start | bytes 22020096 | tf_op jit(solution)/shard_map/all_to_all | solution.py:67
  285.2 452.6 %reduce-scatter.2.cloned.1.call-start = ((), (), s32[]{:S(2)}) async-start(), calls=%async_computation.5 | async-start | bytes 3784704 | tf_op jit(solution)/shard_map/reduce_scatter | solution.py:117
  512.5 13.6 %copy-start.3 = (bf16[4,512,224]{1,2,0:T(8,128)(2,1)S(1)}, bf16[4,512,224]{1,2,0:T(8,128)(2,1)}, u32[]{:S(2)}) copy-start(bf16[4,512,224]{1,2,0:T(8,128)(2,1)} %all_gather.22) | copy-start | bytes 2752516
  526.1 3.0 copy-start.6
  526.1 3.4 copy-start.2
  538.6 199.3 %copy-start.1 = (f32[13,56,128]{2,1,0:T(8,128)S(1)}, f32[13,56,128]{2,1,0:T(8,128)}, u32[]{:S(2)}) copy-start(f32[13,56,128]{2,1,0:T(8,128)} %param.14) | copy-start | bytes 1118212
Sparse Core Ops, SparseCore 0:
  11.6 90.2 all-gather.10
  104.2 24.7 all-gather.12
  131.2 111.0 all-gather.6
  245.7 228.1 all-gather.8
  536.2 201.5 reduce-scatter.1
where the time goes:
time: 746 us; the launch traced here: 744 us
  waiting for transfers between devices  391 us (52%)
  blocking collectives  206 us (28%)
  local copies, waits for them, and re-layouts  73 us (10%)
  matrix products  32.2 us (4%)
  starting transfers between devices  20 us (3%)
  between operations  14.7 us (2%)
    all_gather x1, blocking collectives, body(): key_piece = lax.all_gather(prefix_keys, 'dp', axis=0, tiled=True)  195 us
    reduce_scatter x1, waiting for transfers between devices, body(): lax.psum_scatter(lax.dot_general(attention, server_out, (((1,), (1,)), ((...  186 us
    all_gather x1, waiting for transfers between devices, body(): lax.all_gather(merged_qkv, 'dp', axis=0, tiled=True)  97.9 us
    all_gather x1, waiting for transfers between devices, body(): lax.all_gather(up_pick, 'tensor', axis=1, tiled=True)  90.2 us
    all_to_all x2, local copies, waits for them, and re-layouts, body(): lax.all_to_all(rows_qkv, 'tensor', split_axis=1, concat_axis=0, tiled=True)  32.5 us
    all_gather x1, waiting for transfers between devices, body(): lax.all_gather(out_low, 'dp', axis=0, tiled=True)  17.1 us
    unnamed x28, local copies, waits for them, and re-layouts  16 us
  transfers between devices with their start and end apart: 7, of which 4 were waited for; matrix products, arithmetic and copies ran while one was open for 8% of the time, Pallas kernels for 0%

commit v1 on v0

--- a/solution.py
+++ b/solution.py
@@ -3,6 +3,15 @@
 import jax.numpy as jnp
 from jax import lax
 from jax.sharding import PartitionSpec as P
+
+
+def rails_view(tile_in, in_dim):
+    slots = []
+    for _ in range(lax.axis_size("dp")):
+        slots.append(tile_in)
+    far_arr = jnp.stack(slots, 0)
+    piece_now = lax.all_to_all(far_arr, axis_name="dp", split_axis=0, concat_axis=0)
+    return jnp.concatenate(piece_now, in_dim)
 
 
 def partial_attention(queries, key_rows, value_rows, allowed, inv_scale):
@@ -61,7 +70,7 @@
     out_low = out_master.astype(jnp.bfloat16)
     rows_qkv, rows_out = (
         lax.all_gather(merged_qkv, "dp", axis=0, tiled=True),
-        lax.all_gather(out_low, "dp", axis=0, tiled=True),
+        rails_view(out_low, 0),
     )
     cols_qkv, cols_out = (
         lax.all_to_all(rows_qkv, "tensor", split_axis=1, concat_axis=0, tiled=True),

time: 746 us -> 734 us (0.984)
  waiting for transfers between devices: 391 us -> 348 us
  blocking collectives: 206 us -> 247 us
  starting transfers between devices: 20 us -> 11.5 us
    all_to_all x0 -> x1, blocking collectives: none -> 39.4 us  [rails_view(): lax.all_to_all(far_arr, axis_name='dp', split_axis=0, concat_axis=0)]
    all_gather x1, waiting for transfers between devices: 97.9 us -> 70.7 us  [body(): lax.all_gather(merged_qkv, 'dp', axis=0, tiled=True)]
    all_gather x1 -> x0, waiting for transfers between devices: 17.1 us -> none  [body(): lax.all_gather(out_low, 'dp', axis=0, tiled=True)]
    unnamed x28 -> x30, local copies, waits for them, and re-layouts: 16 us -> 16 us
  transfers between devices with their start and end apart: 7 -> 6, of which waited for: 4 -> 3; matrix products, arithmetic and copies ran while one was open for 8% -> 7% of each run, Pallas kernels for 0% -> 0%
where the time goes in v1:
time: 734 us; the launch traced here: 733 us
  waiting for transfers between devices  348 us (47%)
  blocking collectives  247 us (34%)
  local copies, waits for them, and re-layouts  74.4 us (10%)
  matrix products  32.1 us (4%)
  between operations  14.7 us (2%)
  starting transfers between devices  11.5 us (2%)
    all_gather x1, blocking collectives, body(): key_piece = lax.all_gather(prefix_keys, 'dp', axis=0, tiled=True)  196 us
    reduce_scatter x1, waiting for transfers between devices, body(): lax.psum_scatter(lax.dot_general(attention, server_out, (((1,), (1,)), ((...  185 us
    all_gather x1, waiting for transfers between devices, body(): lax.all_gather(up_pick, 'tensor', axis=1, tiled=True)  92.2 us
    all_gather x1, waiting for transfers between devices, body(): lax.all_gather(merged_qkv, 'dp', axis=0, tiled=True)  70.7 us
    all_to_all x1, blocking collectives, rails_view(): lax.all_to_all(far_arr, axis_name='dp', split_axis=0, concat_axis=0)  39.4 us
    all_to_all x2, local copies, waits for them, and re-layouts, body(): lax.all_to_all(rows_qkv, 'tensor', split_axis=1, concat_axis=0, tiled=True)  32.3 us
    unnamed x30, local copies, waits for them, and re-layouts  16 us
  transfers between devices with their start and end apart: 6, of which 3 were waited for; matrix products, arithmetic and copies ran while one was open for 7% of the time, Pallas kernels for 0%

profile of v1, /device:TPU:0, one launch (start us, length us, event | category | flops | bytes accessed | tf_op | source)
XLA Modules:
  0.0 732.9 jit_solution(4200196415977189575)
XLA Ops:
  7.9 1.7 dynamic-slice_convert_fusion
  9.7 92.2 %all-gather.9.cloned.1.call-done = bf16[1,128,21504]{1,2,0:T(8,128)(2,1)} async-done(((bf16[1,128,672]{1,2,0:T(8,128)(2,1)}), bf16[1,128,21504]{1,2,0:T(8,128)(2,1)}) %all-gather.9.cloned.1.call-update) | async-done | bytes 5505040 | tf_op jit(solution)/shard_map/all_gather | solution.py:65
  101.9 8.7 %fusion = bf16[56,21504]{1,0:T(8,128)(2,1)} fusion(f32[56,21504]{1,0:T(8,128)} %param.13, bf16[1,128,21504]{1,2,0:T(8,128)(2,1)} %all-gather.9.cloned.1.call-done, f32[13,56,128]{2,1,0:T(8,128)S(1)} %copy-done, s32[]{:T(128)S(6)} %select_n.46), kind=kOutput, calls=%fused_computation.1 | convolution fusion | flops 310689792 | bytes 12744708 | tf_op jit(solution)/shard_map/dot_general | solution.py:68
  110.9 0.8 fusion.28
  112.0 39.4 %all_to_all.37 = bf16[4,28,7168]{2,1,0:T(8,128)(2,1)S(1)} all-to-all(bf16[4,28,7168]{2,1,0:T(8,128)(2,1)S(1)} %stack.2), channel_id=1, replica_groups=mesh['dp'=4,'tensor'=32] {'dp'}, dimensions={0} | all-to-all | bytes 3211264 | tf_op jit(solution)/shard_map/all_to_all | solution.py:13
  151.4 3.6 all_to_all.31
  155.0 3.8 copy.29
  158.7 4.7 all-to-all-start.2
  163.5 70.7 %all-gather.5.cloned.1.call-done = bf16[224,21504]{1,0:T(8,128)(2,1)} async-done(((bf16[56,21504]{1,0:T(8,128)(2,1)}), bf16[224,21504]{1,0:T(8,128)(2,1)}) %all-gather.5.cloned.1.call-update) | async-done | bytes 9633808 | tf_op jit(solution)/shard_map/all_gather | solution.py:72
  234.2 20.8 %all_to_all.27 = bf16[224,32,672]{2,1,0:T(8,128)(2,1)} reshape(bf16[224,21504]{1,0:T(8,128)(2,1)} %all-gather.5.cloned.1.call-done) | data formatting | bytes 19267584 | tf_op jit(solution)/shard_map/all_to_all | solution.py:76
  255.1 11.5 %copy.27 = bf16[224,32,672]{2,0,1:T(8,128)(2,1)} copy(bf16[224,32,672]{2,1,0:T(8,128)(2,1)} %all_to_all.27) | data formatting | bytes 19267584 | tf_op jit(solution)/shard_map/all_to_all | solution.py:76
  266.6 6.6 all-to-all-start
  273.3 0.6 fusion.40
  273.9 1.3 select_compare_fusion
  275.2 1.3 select_compare_fusion.2
  276.6 0.6 fusion.41
  277.1 1.3 broadcast_select_fusion
  278.5 196.1 %all_gather.18 = bf16[4,512,224]{1,2,0:T(8,128)(2,1)} all-gather(bf16[1,512,224]{1,2,0:T(8,128)(2,1)S(1)} %copy-done.8), channel_id=1, replica_groups=mesh['dp'=4,'tensor'=32] {'dp'}, dimensions={0}, use_global_device_ids=true | all-gather | bytes 1146880 | tf_op jit(solution)/shard_map/all_gather | solution.py:110
  474.6 11.8 %all_gather.19 = bf16[4,512,224]{1,2,0:T(8,128)(2,1)S(1)} all-gather(bf16[1,512,224]{1,2,0:T(8,128)(2,1)S(1)} %copy-done.9), channel_id=1, replica_groups=mesh['dp'=4,'tensor'=32] {'dp'}, dimensions={0}, use_global_device_ids=true | all-gather | bytes 1146880 | tf_op jit(solution)/shard_map/all_gather | solution.py:111
  486.4 0.7 copy.30
  487.0 2.4 copy.31
  489.4 2.8 reshape.103
  492.2 9.8 %copy.28 = bf16[4,32,56,672]{3,2,1,0:T(8,128)(2,1)} copy(bf16[4,32,56,672]{3,2,0,1:T(8,128)(2,1)} %bitcast.5) | data formatting | bytes 19267584 | tf_op jit(solution)/shard_map/transpose | solution.py:35
  502.1 13.6 %convolution_convert_fusion.1 = bf16[512,672]{0,1:T(8,128)(2,1)S(1)} fusion(bf16[512,7168]{1,0:T(8,128)(2,1)} %all-gather.7.cloned.1.call-done, bf16[7168,672]{1,0:T(8,128)(2,1)} %bitcast.70), kind=kOutput, calls=%fused_computation.19 | convolution fusion | flops 4932845568 | bytes 17661952 | tf_op jit(solution)/shard_map/dot_general | solution.py:81
  515.7 1.3 fusion.42
  517.0 0.5 fusion.43
  517.6 0.5 fusion.44
  520.0 1.1 convolution_add_fusion.2
  521.0 4.6 convolution_convert_fusion
  525.6 2.5 copy.33
  528.1 13.5 %copy.32 = bf16[7168,672]{0,1:T(8,128)(2,1)} copy(bf16[7168,672]{1,0:T(8,128)(2,1)} %bitcast.71) | data formatting | bytes 19267584
  541.6 184.8 %reduce-scatter.2.cloned.1.call-done = bf16[16,3584]{1,0:T(8,128)(2,1)} async-done(((bf16[512,3584]{1,0:T(8,128)(2,1)}), bf16[16,3584]{1,0:T(8,128)(2,1)}) %reduce-scatter.2.cloned.1.call-update) | async-done | bytes 114704 | tf_op jit(solution)/shard_map/reduce_scatter | solution.py:126
  (51 shorter events, 2.6 us)
Async XLA Ops:
  7.2 94.8 %copy-start = (f32[13,56,128]{2,1,0:T(8,128)S(1)}, f32[13,56,128]{2,1,0:T(8,128)}, u32[]{:S(2)}) copy-start(f32[13,56,128]{2,1,0:T(8,128)} %param.14) | copy-start | bytes 1118212
  7.2 94.7 %all-gather.9.cloned.1.call-start = ((), (), s32[]{:S(2)}) async-start(), calls=%async_computation.7 | async-start | bytes 5677056 | tf_op jit(solution)/shard_map/all_gather | solution.py:65
  9.6 101.1 %copy-start.5 = (bf16[16,3584]{1,0:T(8,128)(2,1)S(1)}, bf16[16,3584]{1,0:T(8,128)(2,1)}, u32[]{:S(2)}) copy-start(bf16[16,3584]{1,0:T(8,128)(2,1)} %param.20) | copy-start | bytes 344068
  9.6 101.1 %copy-start.6 = (bf16[16,3584]{1,0:T(8,128)(2,1)S(1)}, bf16[16,3584]{1,0:T(8,128)(2,1)}, u32[]{:S(2)}) copy-start(bf16[16,3584]{1,0:T(8,128)(2,1)} %param.19) | copy-start | bytes 344068
  9.6 101.3 %copy-start.10 = (f32[7168]{0:T(1024)S(1)}, f32[7168]{0:T(1024)}, u32[]{:S(2)}) copy-start(f32[7168]{0:T(1024)} %param.18) | copy-start | bytes 86020
  9.6 102.1 %copy-start.3 = (f32[28,7168]{1,0:T(8,128)S(1)}, f32[28,7168]{1,0:T(8,128)}, u32[]{:S(2)}) copy-start(f32[28,7168]{1,0:T(8,128)} %param.17) | copy-start | bytes 2408452
  9.7 224.6 %all-gather.5.cloned.1.call-start = ((), (), s32[]{:S(2)}) async-start(), calls=%async_computation.4 | async-start | bytes 12042240 | tf_op jit(solution)/shard_map/all_gather | solution.py:72
  110.7 391.4 %all-gather.7.cloned.1.call-start = ((), (), s32[]{:S(2)}) async-start(), calls=%async_computation.5 | async-start | bytes 7569408 | tf_op jit(solution)/shard_map/all_gather | solution.py:64
  158.7 107.8 %all-to-all-start.2 = ((bf16[112,32,224]{2,0,1:T(8,128)(2,1)}), bf16[112,32,224]{2,0,1:T(8,128)(2,1)S(1)}, u32[]{:S(2)}, u32[]{:S(2)}) async-start(bf16[112,32,224]{2,0,1:T(8,128)(2,1)} %copy.29), calls=%async_computation.2 | async-start | bytes 3670016 | tf_op jit(solution)/shard_map/all_to_all | solution.py:77
  266.6 6.7 copy-start.12
  266.6 7.3 copy-start.11
  266.6 10.0 %copy-start.13 = (s32[1,2]{1,0:T(1,128)S(1)}, s32[1,2]{1,0:T(1,128)}, u32[]{:S(2)}) copy-start(s32[1,2]{1,0:T(1,128)} %param.22) | copy-start | bytes 28
  266.6 11.9 %copy-start.8 = (bf16[1,512,224]{1,2,0:T(8,128)(2,1)S(1)}, bf16[1,512,224]{1,2,0:T(8,128)(2,1)}, u32[]{:S(2)}) copy-start(bf16[1,512,224]{1,2,0:T(8,128)(2,1)} %param.24) | copy-start | bytes 688132
  266.6 208.0 %copy-start.9 = (bf16[1,512,224]{1,2,0:T(8,128)(2,1)S(1)}, bf16[1,512,224]{1,2,0:T(8,128)(2,1)}, u32[]{:S(2)}) copy-start(bf16[1,512,224]{1,2,0:T(8,128)(2,1)} %param.25) | copy-start | bytes 688132
  266.6 225.6 %all-to-all-start = ((bf16[224,32,672]{2,0,1:T(8,128)(2,1)}), bf16[224,32,672]{2,0,1:T(8,128)(2,1)}, u32[]{:S(2)}, u32[]{:S(2)}) async-start(bf16[224,32,672]{2,0,1:T(8,128)(2,1)} %copy.27), calls=%async_computation | async-start | bytes 22020096 | tf_op jit(solution)/shard_map/all_to_all | solution.py:76
  273.2 453.1 %reduce-scatter.2.cloned.1.call-start = ((), (), s32[]{:S(2)}) async-start(), calls=%async_computation.6 | async-start | bytes 3784704 | tf_op jit(solution)/shard_map/reduce_scatter | solution.py:126
  502.1 13.6 %copy-start.4 = (bf16[4,512,224]{1,2,0:T(8,128)(2,1)S(1)}, bf16[4,512,224]{1,2,0:T(8,128)(2,1)}, u32[]{:S(2)}) copy-start(bf16[4,512,224]{1,2,0:T(8,128)(2,1)} %all_gather.18) | copy-start | bytes 2752516
  515.7 3.0 copy-start.7
  515.7 3.4 copy-start.2
  528.1 198.2 %copy-start.1 = (f32[13,56,128]{2,1,0:T(8,128)S(1)}, f32[13,56,128]{2,1,0:T(8,128)}, u32[]{:S(2)}) copy-start(f32[13,56,128]{2,1,0:T(8,128)} %param.14) | copy-start | bytes 1118212
Sparse Core Ops, SparseCore 0:
  11.6 90.2 all-gather.8
  110.8 123.3 all-gather.4
  237.8 226.8 all-gather.6
  525.8 200.5 reduce-scatter.1
